TPU v7x, 512 devices: a whole 4x4x16 slice. The times are simulated.
512 devices in a mesh: dp: 64 (over x, z_hi, y, core), bfly: 8 (over z_lo).
Axes of the slice: x: 4, y: 4, z: 16 (z_hi: 2, z_lo: 8; z = z_hi * 8 + z_lo), core: 2. Of those that a mesh axis runs over, the one named last changes fastest.
Arguments:
- features: bfloat16 [8192, 8192], P('dp', 'bfly'), may hold values from -6 to 6
- weight: bfloat16 [4, 256, 14336], P(None, 'dp', 'bfly'), may hold values from -0.1875 to 0.1875
- block_table: int32 [4, 56], P(None, 'bfly'), may hold values from 0 to 3
- upstream: bfloat16 [8192, 14336], P('dp', 'bfly'), may hold values from -6 to 6
Outputs:
- activation: bfloat16 [8192, 14336], P('dp', 'bfly')
- input_grad: bfloat16 [8192, 8192], P('dp', 'bfly')
- weight_grad: float32 [4, 256, 14336], P(None, 'dp', 'bfly')
Inputs may be any that keep to these rules, and one draw needn't show every extreme that they name: block_table[s, k] names a feature block within the partner group of hidden block k at section s.
All inputs are finite; a program needn't handle non-finite values.
Results may differ from a plain program's by a relative error of at most 0.0058.
Values may be sent and summed in bfloat16 or wider, within the bound.
No kernel may reach another device: no remote copies, remote signals or barrier semaphores. Data moves between devices by JAX's collectives and lax.ppermute only.
A program may use at most 64 MiB of HBM per device.

v0:
```python
import jax
import jax.numpy as jnp
from jax import lax
from jax.experimental import pallas as pl
from jax.experimental.pallas import tpu as pltpu
from jax.sharding import Mesh
from jax.sharding import PartitionSpec as P


half_root = 0.7071067811865476
inv_root_tau = 0.3989422804014327
XS, ZS, YS, CS = 4, 2, 4, 2
DP = ("x", "zh", "y", "core")
PLANE = ("x", "y")
VMEM_LIMIT = 14 * 1024 * 1024


def swapped(block, stride):
    count = lax.axis_size("bfly")
    return lax.ppermute(block, "bfly", [(low, low ^ (1 << stride)) for low in range(count)])


def flipped(block, axis):
    return lax.ppermute(block, axis, [(0, 1), (1, 0)])


def vmem():
    return pl.BlockSpec(memory_space=pltpu.VMEM)


def smem():
    return pl.BlockSpec(memory_space=pltpu.SMEM)


def params(limit=VMEM_LIMIT):
    return pltpu.CompilerParams(vmem_limit_bytes=limit)


def columns_of(block):
    return pl.ds(pl.multiple_of(block * 256, 256), 256)


def grid_of(rows):
    return tuple(lax.broadcasted_iota(jnp.int32, (rows, 256), axis) for axis in (0, 1))


def natural(section, z, y, core, row):
    return section * 64 + z * 32 + y * 8 + core * 4 + row


def gather_order():
    core, half = lax.axis_index("core"), lax.axis_index("zh")
    row, col = grid_of(256)
    stored = natural((col >> 2) & 3, ((col >> 6) & 1) ^ half, (col >> 4) & 3, (col >> 7) ^ core, col & 3)
    return (row == stored).astype(jnp.bfloat16)


def scatter_order():
    row, col = grid_of(128)
    sent = natural((row >> 2) & 3, row >> 6, (row >> 4) & 3, lax.axis_index("core"), row & 3)
    return (col == sent).astype(jnp.bfloat16)


def forward_kernel(tab, f0, f1, f2, f3, w00, w01, w10, w11, up_hbm, act, pack, wn, up, sem):
    feats = (f0, f1, f2, f3)
    sections, hidden_blocks = tab.shape
    fetch = pltpu.make_async_copy(up_hbm, up, sem)
    fetch.start()
    order = gather_order()
    for x in range(XS):
        rows = jnp.concatenate([w00[x], w01[x], w10[x], w11[x]], axis=0)
        ordered = jnp.dot(order, rows, preferred_element_type=jnp.float32).astype(jnp.bfloat16)
        for s in range(sections):
            wn[s, x * 64 : (x + 1) * 64, :] = ordered[s * 64 : (s + 1) * 64]
    edge = f3.shape[1]
    pack[:, :edge] = f3[...]
    fetch.wait()
    for j in range(hidden_blocks):
        cols = slice(j * 256, (j + 1) * 256)
        spot = slice(edge + j * 256, edge + (j + 1) * 256)
        pre = None
        for s in range(sections):
            term = jnp.dot(feats[s][:, columns_of(tab[s, j])], wn[s, :, cols], preferred_element_type=jnp.float32)
            pre = term if pre is None else pre + term
        cdf = 0.5 * (1.0 + lax.erf(pre * half_root))
        density = jnp.exp(-0.5 * pre * pre) * inv_root_tau
        act[:, cols] = (pre * cdf).astype(jnp.bfloat16)
        pack[:, spot] = (up[:, cols].astype(jnp.float32) * (cdf + pre * density)).astype(jnp.bfloat16)


def halved(into, rows):
    for x in range(XS):
        for z in range(ZS):
            start = x * 64 + z * 32
            into[z, x * 32 : (x + 1) * 32] = rows[start : start + 32]


def turn_kernel(f0, f1, f2, ft):
    for s, feats in enumerate((f0, f1, f2)):
        for b in range(4):
            halved(ft.at[s, b], feats[:, b * 256 : (b + 1) * 256].T)


def weight_rows(z, tab, ft0, ft1, last, pack0, pack1, out, terms):
    sections, hidden_blocks = tab.shape
    edge = last.shape[0] * 256
    for j in range(hidden_blocks):
        cols = slice(j * 256, (j + 1) * 256)
        spot = slice(edge + j * 256, edge + (j + 1) * 256)
        grad = jnp.concatenate([pack0[:, spot], pack1[:, spot]], axis=0)
        for s in range(sections):
            b = tab[s, j]
            turned = jnp.concatenate([ft0[s, b, z], ft1[s, b, z]], axis=1) if s < sections - 1 else last[b, z]
            term = jnp.dot(turned, grad, preferred_element_type=jnp.float32).astype(jnp.bfloat16)
            for pair in range(2):
                terms[pair, s * 64 : (s + 1) * 64, cols] = term[pair * 64 : (pair + 1) * 64]
    order = scatter_order()
    for pair in range(2):
        out[pair] = jnp.dot(order, terms[pair], preferred_element_type=jnp.float32).astype(jnp.bfloat16)


def far_kernel(tab, ft0, ft1, pack0, pack1, out, last, terms):
    for b in range(4):
        cols = slice(b * 256, (b + 1) * 256)
        halved(last.at[b], jnp.concatenate([pack0[:, cols].T, pack1[:, cols].T], axis=1))
    weight_rows(1 - lax.axis_index("zh"), tab, ft0, ft1, last, pack0, pack1, out, terms)


def near_kernel(tab, ft0, ft1, last, pack0, pack1, out, terms):
    weight_rows(lax.axis_index("zh"), tab, ft0, ft1, last, pack0, pack1, out, terms)


def share_kernel(tab, pack, wn, s0, s1, s2, s3, total):
    shares = (s0, s1, s2, s3)
    edge = s0.shape[1]
    sections, hidden_blocks = tab.shape
    for s in range(sections):
        total[...] = jnp.zeros_like(total)
        for j in range(hidden_blocks):
            cols = slice(j * 256, (j + 1) * 256)
            spot = slice(edge + j * 256, edge + (j + 1) * 256)
            place = columns_of(tab[s, j])
            total[:, place] += lax.dot_general(
                pack[:, spot], wn[s, :, cols], (((1,), (1,)), ((), ())), preferred_element_type=jnp.float32
            )
        shares[s][...] = total[...].astype(jnp.bfloat16)


def repeat_kernel(shard, out):
    for peer in range(out.shape[0]):
        out[peer] = shard[...]


def exchanged(rows):
    return lax.all_to_all(rows, PLANE, split_axis=0, concat_axis=0, tiled=True)


def spread(shard):
    everyone = pl.pallas_call(
        repeat_kernel,
        out_shape=jax.ShapeDtypeStruct((XS * YS, *shard.shape), shard.dtype),
        in_specs=[vmem()],
        out_specs=vmem(),
        compiler_params=params(4 * 1024 * 1024),
        name="repeat",
    )(shard)
    got = exchanged(everyone)
    return got.reshape(XS, YS * shard.shape[0], shard.shape[1])


def body(features, weight, block_table, upstream):
    tok_rows = features.shape[0]
    sections, shard_rows, width = weight.shape
    bf16 = jnp.bfloat16
    shard = weight.reshape(sections * shard_rows, width)
    w00 = spread(shard)
    far = flipped(shard, "zh")
    feats = [features]
    for bit in range(3):
        feats.append(swapped(features, bit))
    w10 = flipped(w00, "core")
    w01 = spread(far)
    w11 = flipped(w01, "core")

    turned = pl.pallas_call(
        turn_kernel,
        out_shape=jax.ShapeDtypeStruct((sections - 1, 4, ZS, 128, tok_rows), bf16),
        in_specs=[vmem()] * 3,
        out_specs=vmem(),
        compiler_params=params(),
        name="turn",
    )(*feats[:3])
    turned_got = flipped(turned, "core")

    edge = features.shape[1]
    act, pack, wn = pl.pallas_call(
        forward_kernel,
        out_shape=(
            jax.ShapeDtypeStruct((tok_rows, width), bf16),
            jax.ShapeDtypeStruct((tok_rows, edge + width), bf16),
            jax.ShapeDtypeStruct((sections, 256, width), bf16),
        ),
        in_specs=[smem()] + [vmem()] * 8 + [pl.BlockSpec(memory_space=pltpu.MemorySpace.HBM)],
        out_specs=(vmem(), vmem(), vmem()),
        scratch_shapes=[pltpu.VMEM((tok_rows, width), bf16), pltpu.SemaphoreType.DMA],
        compiler_params=params(),
        name="forward",
    )(block_table, *feats, w00, w01, w10, w11, upstream)
    pack_got = flipped(pack, "core")

    share = jax.ShapeDtypeStruct((tok_rows, edge), bf16)
    shares = pl.pallas_call(
        share_kernel,
        out_shape=(share,) * 4,
        in_specs=[smem()] + [vmem()] * 2,
        out_specs=(vmem(),) * 4,
        scratch_shapes=[pltpu.VMEM((tok_rows, edge), jnp.float32)],
        compiler_params=params(),
        name="shares",
    )(block_table, pack, wn)

    rows_shape = jax.ShapeDtypeStruct((2, 128, width), bf16)
    last_shape = jax.ShapeDtypeStruct((4, ZS, 128, 2 * tok_rows), bf16)
    terms = [pltpu.VMEM((2, 256, width), bf16)]
    far_rows, last = pl.pallas_call(
        far_kernel,
        out_shape=(rows_shape, last_shape),
        in_specs=[smem()] + [vmem()] * 4,
        out_specs=(vmem(), vmem()),
        scratch_shapes=terms,
        compiler_params=params(),
        name="far_rows",
    )(block_table, turned, turned_got, pack, pack_got)
    far_got = exchanged(far_rows.reshape(XS * YS, 16, width))
    near_rows = pl.pallas_call(
        near_kernel,
        out_shape=rows_shape,
        in_specs=[smem()] + [vmem()] * 5,
        out_specs=vmem(),
        scratch_shapes=terms,
        compiler_params=params(),
        name="near_rows",
    )(block_table, turned, turned_got, last, pack, pack_got)
    arrived = []
    for bit in range(3):
        arrived.append(swapped(shares[bit + 1], bit))
    near_got = exchanged(near_rows.reshape(XS * YS, 16, width))
    far_sum = jnp.sum(far_got.astype(jnp.float32), axis=0).astype(bf16)
    other = flipped(far_sum, "zh")
    mine = jnp.sum(near_got.astype(jnp.float32), axis=0)
    scale = float(tok_rows * XS * ZS * YS * CS) ** -0.5
    weight_grad = ((mine + other.astype(jnp.float32)) * scale).reshape(sections, shard_rows, width)

    input_grad = shares[0].astype(jnp.float32)
    for part in arrived:
        input_grad = input_grad + part.astype(jnp.float32)
    input_grad = input_grad.astype(bf16)
    return act, input_grad, weight_grad


def solution(mesh):
    fine = Mesh(mesh.devices.reshape(XS, ZS, YS, CS, mesh.shape["bfly"]), (*DP, "bfly"))
    return jax.shard_map(
        body,
        mesh=fine,
        in_specs=(P(DP, "bfly"), P(None, DP, "bfly"), P(None, "bfly"), P(DP, "bfly")),
        out_specs=(P(DP, "bfly"), P(DP, "bfly"), P(None, DP, "bfly")),
        check_vma=False,
    )
```

profile of v0, /device:TPU:66, one launch (start us, length us, event | category | flops | bytes accessed | tf_op | source)
XLA Modules:
  0.0 183.3 jit_solution(12808403412634682391)
XLA Ops:
  0.6 0.0 copy-start.4
  0.6 0.0 copy-start.7
  0.7 0.9 reshape.24.shard
  1.5 1.0 repeat.2
  2.6 7.5 %all-to-all-start = ((bf16[16,16,1792]{2,1,0:T(8,128)(2,1)}), bf16[16,16,1792]{2,1,0:T(8,128)(2,1)S(1)}, u32[]{:S(2)}, u32[]{:S(2)}) async-start(bf16[16,16,1792]{2,1,0:T(8,128)(2,1)} %repeat.2), calls=%async_computation | async-start | bytes 1835008 | tf_op jit(solution)/shard_map/all_to_all | solution.py:155
  10.0 13.9 %collective-permute-start.3 = (bf16[16,1792]{1,0:T(8,128)(2,1)S(1)}, bf16[16,1792]{1,0:T(8,128)(2,1)S(1)}, u32[]{:S(2)}, u32[]{:S(2)}) collective-permute-start(bf16[16,1792]{1,0:T(8,128)(2,1)S(1)} %reshape.24.shard), channel_id=1, source_target_pairs={{0,64},{64,0},{1,65},{65,1},{2,66},{66,2},{3,67},{67,3},{4,68},{68... | collective-permute-start | bytes 172040 | tf_op jit(solution)/shard_map/ppermute | solution.py:24
  24.0 2.4 %collective-permute-done.3.shard = bf16[16,1792]{1,0:T(8,128)(2,1)S(1)} collective-permute-done((bf16[16,1792]{1,0:T(8,128)(2,1)S(1)}, bf16[16,1792]{1,0:T(8,128)(2,1)S(1)}, u32[]{:S(2)}, u32[]{:S(2)}) %collective-permute-start.3) | collective-permute-done | bytes 57376 | tf_op jit(solution)/shard_map/ppermute | solution.py:24
  26.4 1.0 repeat.3
  27.4 0.0 all-to-all-done
  27.4 7.2 %all-to-all-start.1 = ((bf16[16,16,1792]{2,1,0:T(8,128)(2,1)}), bf16[16,16,1792]{2,1,0:T(8,128)(2,1)S(1)}, u32[]{:S(2)}, u32[]{:S(2)}) async-start(bf16[16,16,1792]{2,1,0:T(8,128)(2,1)} %repeat.3), calls=%async_computation.1 | async-start | bytes 1835008 | tf_op jit(solution)/shard_map/all_to_all | solution.py:155
  34.6 1.9 %collective-permute-start.4 = (bf16[4,64,1792]{2,1,0:T(8,128)(2,1)S(1)}, bf16[4,64,1792]{2,1,0:T(8,128)(2,1)}, u32[]{:S(2)}, u32[]{:S(2)}) collective-permute-start(bf16[4,64,1792]{2,1,0:T(8,128)(2,1)S(1)} %bitcast.4), channel_id=1, source_target_pairs={{0,8},{8,0},{1,9},{9,1},{2,10},{10,2},{3,11},{11,3},{4,12},{12,4},... | collective-permute-start | bytes 2752520 | tf_op jit(solution)/shard_map/ppermute | solution.py:24
  36.5 10.0 %all-to-all-done.1 = bf16[16,16,1792]{2,1,0:T(8,128)(2,1)S(1)} async-done(((bf16[16,16,1792]{2,1,0:T(8,128)(2,1)}), bf16[16,16,1792]{2,1,0:T(8,128)(2,1)S(1)}, u32[]{:S(2)}, u32[]{:S(2)}) %all-to-all-start.1) | async-done | bytes 917536 | tf_op jit(solution)/shard_map/all_to_all | solution.py:155
  46.5 1.9 %collective-permute-start.5 = (bf16[4,64,1792]{2,1,0:T(8,128)(2,1)S(1)}, bf16[4,64,1792]{2,1,0:T(8,128)(2,1)S(1)}, u32[]{:S(2)}, u32[]{:S(2)}) collective-permute-start(bf16[4,64,1792]{2,1,0:T(8,128)(2,1)S(1)} %bitcast.6), channel_id=1, source_target_pairs={{0,8},{8,0},{1,9},{9,1},{2,10},{10,2},{3,11},{11,3},{4,12},{12,4},... | collective-permute-start | bytes 2752520 | tf_op jit(solution)/shard_map/ppermute | solution.py:24
  48.4 0.0 copy-done.4
  48.5 3.0 %collective-permute-start = (bf16[128,1024]{1,0:T(8,128)(2,1)S(1)}, bf16[128,1024]{1,0:T(8,128)(2,1)S(1)}, u32[]{:S(2)}, u32[]{:S(2)}) collective-permute-start(bf16[128,1024]{1,0:T(8,128)(2,1)S(1)} %copy-done.4), channel_id=1, source_target_pairs={{0,1},{1,0},{2,3},{3,2},{4,5},{5,4},{6,7},{7,6},{8,9},{9,8},{10,11... | collective-permute-start | bytes 786440 | tf_op jit(solution)/shard_map/ppermute | solution.py:20
  51.5 3.2 %collective-permute-start.1 = (bf16[128,1024]{1,0:T(8,128)(2,1)S(1)}, bf16[128,1024]{1,0:T(8,128)(2,1)S(1)}, u32[]{:S(2)}, u32[]{:S(2)}) collective-permute-start(bf16[128,1024]{1,0:T(8,128)(2,1)S(1)} %copy-done.4), channel_id=1, source_target_pairs={{0,2},{1,3},{2,0},{3,1},{4,6},{5,7},{6,4},{7,5},{8,10},{9,11},{10,... | collective-permute-start | bytes 786440 | tf_op jit(solution)/shard_map/ppermute | solution.py:20
  54.7 8.5 %collective-permute-start.2 = (bf16[128,1024]{1,0:T(8,128)(2,1)S(1)}, bf16[128,1024]{1,0:T(8,128)(2,1)S(1)}, u32[]{:S(2)}, u32[]{:S(2)}) collective-permute-start(bf16[128,1024]{1,0:T(8,128)(2,1)S(1)} %copy-done.4), channel_id=1, source_target_pairs={{0,4},{1,5},{2,6},{3,7},{4,0},{5,1},{6,2},{7,3},{8,12},{9,13},{10,... | collective-permute-start | bytes 786440 | tf_op jit(solution)/shard_map/ppermute | solution.py:20
  63.2 0.0 collective-permute-done.f1
  63.2 11.4 %collective-permute-done.1.f2 = bf16[128,1024]{1,0:T(8,128)(2,1)S(1)} collective-permute-done((bf16[128,1024]{1,0:T(8,128)(2,1)S(1)}, bf16[128,1024]{1,0:T(8,128)(2,1)S(1)}, u32[]{:S(2)}, u32[]{:S(2)}) %collective-permute-start.1) | collective-permute-done | bytes 262176 | tf_op jit(solution)/shard_map/ppermute | solution.py:20
  74.7 0.3 turn.1.ft0
  74.9 1.9 %collective-permute-start.9 = (bf16[3,4,2,128,128]{4,3,2,1,0:T(8,128)(2,1)S(1)}, bf16[3,4,2,128,128]{4,3,2,1,0:T(8,128)(2,1)S(1)}, u32[]{:S(2)}, u32[]{:S(2)}) collective-permute-start(bf16[3,4,2,128,128]{4,3,2,1,0:T(8,128)(2,1)S(1)} %turn.1.ft0), channel_id=1, source_target_pairs={{0,8},{8,0},{1,9},{9,1},{2,10},{10,2},{3,11},{11,3},{4,12},{12,4},... | collective-permute-start | bytes 2359304 | tf_op jit(solution)/shard_map/ppermute | solution.py:24
  76.9 8.2 %collective-permute-done.2.f3 = bf16[128,1024]{1,0:T(8,128)(2,1)S(1)} collective-permute-done((bf16[128,1024]{1,0:T(8,128)(2,1)S(1)}, bf16[128,1024]{1,0:T(8,128)(2,1)S(1)}, u32[]{:S(2)}, u32[]{:S(2)}) %collective-permute-start.2) | collective-permute-done | bytes 262176 | tf_op jit(solution)/shard_map/ppermute | solution.py:20
  85.1 0.0 collective-permute-done.4.w10
  85.1 0.0 collective-permute-done.5.w11
  85.1 0.0 copy-done.7
  85.1 0.0 copy-start.5
  85.1 0.9 copy-done.5
  86.1 0.0 copy-start.6
  86.1 1.0 copy-done.6
  87.1 4.3 %forward.1 = (bf16[128,1792]{1,0:T(8,128)(2,1)}, bf16[128,2816]{1,0:T(8,128)(2,1)S(1)}, bf16[4,256,1792]{2,1,0:T(8,128)(2,1)S(1)}) custom-call(s32[4,7]{1,0:T(4,128)S(1)} %copy-done.7, bf16[128,1024]{1,0:T(8,128)(2,1)S(1)} %copy-done.5, bf16[128,1024]{1,0:T(8,128)(2,1)S(1)} %collective-permute-done.f1, bf16[128,1024]{1,0:T(8,128)(2,1)S(1)} %collective-permute-done.1.f2, ...), custom_call_target="tpu_custom_call" | custom-call | tf_op jit(solution)/shard_map/forward/pallas_call | solution.py:196
  91.4 0.0 copy-start
  91.5 1.8 copy-done
  93.2 1.9 %collective-permute-start.10 = (bf16[128,2816]{1,0:T(8,128)(2,1)S(1)}, bf16[128,2816]{1,0:T(8,128)(2,1)S(1)}, u32[]{:S(2)}, u32[]{:S(2)}) collective-permute-start(bf16[128,2816]{1,0:T(8,128)(2,1)S(1)} %get-tuple-element.13.pack.pack0), channel_id=1, source_target_pairs={{0,8},{8,0},{1,9},{9,1},{2,10},{10,2},{3,11},{11,3},{4,12},{12,4},... | collective-permute-start | bytes 2162696 | tf_op jit(solution)/shard_map/ppermute | solution.py:24
  95.1 0.0 collective-permute-done.9.ft1
  95.2 2.1 %collective-permute-done.10.pack1 = bf16[128,2816]{1,0:T(8,128)(2,1)S(1)} collective-permute-done((bf16[128,2816]{1,0:T(8,128)(2,1)S(1)}, bf16[128,2816]{1,0:T(8,128)(2,1)S(1)}, u32[]{:S(2)}, u32[]{:S(2)}) %collective-permute-start.10) | collective-permute-done | bytes 720928 | tf_op jit(solution)/shard_map/ppermute | solution.py:24
  97.3 2.5 %far_rows.1 = (bf16[2,128,1792]{2,1,0:T(8,128)(2,1)}, bf16[4,2,128,256]{3,2,1,0:T(8,128)(2,1)S(1)}) custom-call(s32[4,7]{1,0:T(4,128)S(1)} %copy-done.7, bf16[3,4,2,128,128]{4,3,2,1,0:T(8,128)(2,1)S(1)} %turn.1.ft0, bf16[3,4,2,128,128]{4,3,2,1,0:T(8,128)(2,1)S(1)} %collective-permute-done.9.ft1, bf16[128,2816]{1,0:T(8,128)(2,1)S(1)} %get-tuple-element.13.pack.pack0, ...), custom_call_target="tpu_custom_call" | custom-call | tf_op jit(solution)/shard_map/far_rows/pallas_call | solution.py:225
  99.8 0.0 copy-start.2
  99.8 0.9 copy-done.2
  100.7 6.7 %all-to-all-start.3 = ((bf16[16,16,1792]{2,1,0:T(8,128)(2,1)}), bf16[16,16,1792]{2,1,0:T(8,128)(2,1)}, u32[]{:S(2)}, u32[]{:S(2)}) async-start(bf16[16,16,1792]{2,1,0:T(8,128)(2,1)} %bitcast.3), calls=%async_computation.3 | async-start | bytes 1835008 | tf_op jit(solution)/shard_map/all_to_all | solution.py:155
  107.4 0.0 copy-start.3
  107.4 1.1 copy-done.3
  108.5 2.4 %near_rows.1 = bf16[2,128,1792]{2,1,0:T(8,128)(2,1)} custom-call(s32[4,7]{1,0:T(4,128)S(1)} %copy-done.7, bf16[3,4,2,128,128]{4,3,2,1,0:T(8,128)(2,1)S(1)} %turn.1.ft0, bf16[3,4,2,128,128]{4,3,2,1,0:T(8,128)(2,1)S(1)} %copy-done.3, bf16[4,2,128,256]{3,2,1,0:T(8,128)(2,1)S(1)} %get-tuple-element.19.last, bf16[128,2816]{1,0:T(8,128)(2,1)S(1)} %get-tuple-element.13.pack.pack0, ...), custom_call_target="tpu_custom_call" | custom-call | tf_op jit(solution)/shard_map/near_rows/pallas_call | solution.py:235
  111.0 10.7 %all-to-all-done.3 = bf16[16,16,1792]{2,1,0:T(8,128)(2,1)} async-done(((bf16[16,16,1792]{2,1,0:T(8,128)(2,1)}), bf16[16,16,1792]{2,1,0:T(8,128)(2,1)}, u32[]{:S(2)}, u32[]{:S(2)}) %all-to-all-start.3) | async-done | bytes 917536 | tf_op jit(solution)/shard_map/all_to_all | solution.py:155
  121.7 6.2 %all-to-all-start.2 = ((bf16[16,16,1792]{2,1,0:T(8,128)(2,1)}), bf16[16,16,1792]{2,1,0:T(8,128)(2,1)S(1)}, u32[]{:S(2)}, u32[]{:S(2)}) async-start(bf16[16,16,1792]{2,1,0:T(8,128)(2,1)} %bitcast.2), calls=%async_computation.2 | async-start | bytes 1835008 | tf_op jit(solution)/shard_map/all_to_all | solution.py:155
  127.9 0.0 copy-start.1
  127.9 2.0 %copy-done.1 = bf16[4,256,1792]{2,1,0:T(8,128)(2,1)S(1)} copy-done((bf16[4,256,1792]{2,1,0:T(8,128)(2,1)S(1)}, bf16[4,256,1792]{2,1,0:T(8,128)(2,1)}, u32[]{:S(2)}) %copy-start.1) | copy-done | bytes 3670040
  129.9 2.1 %shares.1 = (bf16[128,1024]{1,0:T(8,128)(2,1)S(1)}, bf16[128,1024]{1,0:T(8,128)(2,1)S(1)}, bf16[128,1024]{1,0:T(8,128)(2,1)S(1)}, bf16[128,1024]{1,0:T(8,128)(2,1)S(1)}) custom-call(s32[4,7]{1,0:T(4,128)S(1)} %copy-done.7, bf16[128,2816]{1,0:T(8,128)(2,1)S(1)} %get-tuple-element.13.pack.pack0, bf16[4,256,1792]{2,1,0:T(8,128)(2,1)S(1)} %copy-done.1), custom_call_target="tpu_custom_call" | custom-call | tf_op jit(solution)/shard_map/shares/pallas_call | solution.py:212
  132.0 6.5 %collective-permute-start.8 = (bf16[128,1024]{1,0:T(8,128)(2,1)S(1)}, bf16[128,1024]{1,0:T(8,128)(2,1)S(1)}, u32[]{:S(2)}, u32[]{:S(2)}) collective-permute-start(bf16[128,1024]{1,0:T(8,128)(2,1)S(1)} %get-tuple-element.18), channel_id=1, source_target_pairs={{0,4},{1,5},{2,6},{3,7},{4,0},{5,1},{6,2},{7,3},{8,12},{9,13},{10,... | collective-permute-start | bytes 786440 | tf_op jit(solution)/shard_map/ppermute | solution.py:20
  138.5 1.9 %collective-permute-start.7 = (bf16[128,1024]{1,0:T(8,128)(2,1)S(1)}, bf16[128,1024]{1,0:T(8,128)(2,1)S(1)}, u32[]{:S(2)}, u32[]{:S(2)}) collective-permute-start(bf16[128,1024]{1,0:T(8,128)(2,1)S(1)} %get-tuple-element.17), channel_id=1, source_target_pairs={{0,2},{1,3},{2,0},{3,1},{4,6},{5,7},{6,4},{7,5},{8,10},{9,11},{10,... | collective-permute-start | bytes 786440 | tf_op jit(solution)/shard_map/ppermute | solution.py:20
  140.4 6.6 %collective-permute-start.6 = (bf16[128,1024]{1,0:T(8,128)(2,1)S(1)}, bf16[128,1024]{1,0:T(8,128)(2,1)S(1)}, u32[]{:S(2)}, u32[]{:S(2)}) collective-permute-start(bf16[128,1024]{1,0:T(8,128)(2,1)S(1)} %get-tuple-element.16), channel_id=1, source_target_pairs={{0,1},{1,0},{2,3},{3,2},{4,5},{5,4},{6,7},{7,6},{8,9},{9,8},{10,11... | collective-permute-start | bytes 786440 | tf_op jit(solution)/shard_map/ppermute | solution.py:20
  147.0 11.3 %collective-permute-done.8 = bf16[128,1024]{1,0:T(8,128)(2,1)S(1)} collective-permute-done((bf16[128,1024]{1,0:T(8,128)(2,1)S(1)}, bf16[128,1024]{1,0:T(8,128)(2,1)S(1)}, u32[]{:S(2)}, u32[]{:S(2)}) %collective-permute-start.8) | collective-permute-done | bytes 262176 | tf_op jit(solution)/shard_map/ppermute | solution.py:20
  158.3 0.0 collective-permute-done.7
  158.3 5.1 %collective-permute-done.6 = bf16[128,1024]{1,0:T(8,128)(2,1)S(1)} collective-permute-done((bf16[128,1024]{1,0:T(8,128)(2,1)S(1)}, bf16[128,1024]{1,0:T(8,128)(2,1)S(1)}, u32[]{:S(2)}, u32[]{:S(2)}) %collective-permute-start.6) | collective-permute-done | bytes 262176 | tf_op jit(solution)/shard_map/ppermute | solution.py:20
  163.4 0.9 add_convert_fusion
  164.3 1.3 reduce_sum.22
  165.6 14.8 %collective-permute-start.11 = (bf16[16,1792]{1,0:T(8,128)(2,1)S(1)}, bf16[16,1792]{1,0:T(8,128)(2,1)S(1)}, u32[]{:S(2)}, u32[]{:S(2)}) collective-permute-start(bf16[16,1792]{1,0:T(8,128)(2,1)S(1)} %reduce_sum.22), channel_id=1, source_target_pairs={{0,64},{64,0},{1,65},{65,1},{2,66},{66,2},{3,67},{67,3},{4,68},{68... | collective-permute-start | bytes 172040 | tf_op jit(solution)/shard_map/ppermute | solution.py:24
  180.4 0.0 all-to-all-done.2
  180.5 0.1 convert_reduce_fusion
  180.6 2.0 %collective-permute-done.11 = bf16[16,1792]{1,0:T(8,128)(2,1)S(1)} collective-permute-done((bf16[16,1792]{1,0:T(8,128)(2,1)S(1)}, bf16[16,1792]{1,0:T(8,128)(2,1)S(1)}, u32[]{:S(2)}, u32[]{:S(2)}) %collective-permute-start.11) | collective-permute-done | bytes 57376 | tf_op jit(solution)/shard_map/ppermute | solution.py:24
  182.6 0.7 reshape.29
  (1 shorter events, 0.0 us)
Async XLA Ops:
  0.6 47.8 %copy-start.4 = (bf16[128,1024]{1,0:T(8,128)(2,1)S(1)}, bf16[128,1024]{1,0:T(8,128)(2,1)}, u32[]{:S(2)}) copy-start(bf16[128,1024]{1,0:T(8,128)(2,1)} %f0.3) | copy-start | bytes 786436
  0.6 84.5 %copy-start.7 = (s32[4,7]{1,0:T(4,128)S(1)}, s32[4,7]{1,0:T(4,128)}, u32[]{:S(2)}) copy-start(s32[4,7]{1,0:T(4,128)} %tab.7) | copy-start | bytes 340
  2.6 24.8 %all-to-all-start = ((bf16[16,16,1792]{2,1,0:T(8,128)(2,1)}), bf16[16,16,1792]{2,1,0:T(8,128)(2,1)S(1)}, u32[]{:S(2)}, u32[]{:S(2)}) async-start(bf16[16,16,1792]{2,1,0:T(8,128)(2,1)} %repeat.2), calls=%async_computation | async-start | bytes 1835008 | tf_op jit(solution)/shard_map/all_to_all | solution.py:155
  10.0 16.4 %collective-permute-start.3 = (bf16[16,1792]{1,0:T(8,128)(2,1)S(1)}, bf16[16,1792]{1,0:T(8,128)(2,1)S(1)}, u32[]{:S(2)}, u32[]{:S(2)}) collective-permute-start(bf16[16,1792]{1,0:T(8,128)(2,1)S(1)} %reshape.24.shard), channel_id=1, source_target_pairs={{0,64},{64,0},{1,65},{65,1},{2,66},{66,2},{3,67},{67,3},{4,68},{68... | collective-permute-start | bytes 172040 | tf_op jit(solution)/shard_map/ppermute | solution.py:24
  27.4 19.1 %all-to-all-start.1 = ((bf16[16,16,1792]{2,1,0:T(8,128)(2,1)}), bf16[16,16,1792]{2,1,0:T(8,128)(2,1)S(1)}, u32[]{:S(2)}, u32[]{:S(2)}) async-start(bf16[16,16,1792]{2,1,0:T(8,128)(2,1)} %repeat.3), calls=%async_computation.1 | async-start | bytes 1835008 | tf_op jit(solution)/shard_map/all_to_all | solution.py:155
  34.6 50.5 %collective-permute-start.4 = (bf16[4,64,1792]{2,1,0:T(8,128)(2,1)S(1)}, bf16[4,64,1792]{2,1,0:T(8,128)(2,1)}, u32[]{:S(2)}, u32[]{:S(2)}) collective-permute-start(bf16[4,64,1792]{2,1,0:T(8,128)(2,1)S(1)} %bitcast.4), channel_id=1, source_target_pairs={{0,8},{8,0},{1,9},{9,1},{2,10},{10,2},{3,11},{11,3},{4,12},{12,4},... | collective-permute-start | bytes 2752520 | tf_op jit(solution)/shard_map/ppermute | solution.py:24
  46.5 38.6 %collective-permute-start.5 = (bf16[4,64,1792]{2,1,0:T(8,128)(2,1)S(1)}, bf16[4,64,1792]{2,1,0:T(8,128)(2,1)S(1)}, u32[]{:S(2)}, u32[]{:S(2)}) collective-permute-start(bf16[4,64,1792]{2,1,0:T(8,128)(2,1)S(1)} %bitcast.6), channel_id=1, source_target_pairs={{0,8},{8,0},{1,9},{9,1},{2,10},{10,2},{3,11},{11,3},{4,12},{12,4},... | collective-permute-start | bytes 2752520 | tf_op jit(solution)/shard_map/ppermute | solution.py:24
  48.5 14.8 %collective-permute-start = (bf16[128,1024]{1,0:T(8,128)(2,1)S(1)}, bf16[128,1024]{1,0:T(8,128)(2,1)S(1)}, u32[]{:S(2)}, u32[]{:S(2)}) collective-permute-start(bf16[128,1024]{1,0:T(8,128)(2,1)S(1)} %copy-done.4), channel_id=1, source_target_pairs={{0,1},{1,0},{2,3},{3,2},{4,5},{5,4},{6,7},{7,6},{8,9},{9,8},{10,11... | collective-permute-start | bytes 786440 | tf_op jit(solution)/shard_map/ppermute | solution.py:20
  51.5 23.2 %collective-permute-start.1 = (bf16[128,1024]{1,0:T(8,128)(2,1)S(1)}, bf16[128,1024]{1,0:T(8,128)(2,1)S(1)}, u32[]{:S(2)}, u32[]{:S(2)}) collective-permute-start(bf16[128,1024]{1,0:T(8,128)(2,1)S(1)} %copy-done.4), channel_id=1, source_target_pairs={{0,2},{1,3},{2,0},{3,1},{4,6},{5,7},{6,4},{7,5},{8,10},{9,11},{10,... | collective-permute-start | bytes 786440 | tf_op jit(solution)/shard_map/ppermute | solution.py:20
  54.7 30.4 %collective-permute-start.2 = (bf16[128,1024]{1,0:T(8,128)(2,1)S(1)}, bf16[128,1024]{1,0:T(8,128)(2,1)S(1)}, u32[]{:S(2)}, u32[]{:S(2)}) collective-permute-start(bf16[128,1024]{1,0:T(8,128)(2,1)S(1)} %copy-done.4), channel_id=1, source_target_pairs={{0,4},{1,5},{2,6},{3,7},{4,0},{5,1},{6,2},{7,3},{8,12},{9,13},{10,... | collective-permute-start | bytes 786440 | tf_op jit(solution)/shard_map/ppermute | solution.py:20
  74.9 20.2 %collective-permute-start.9 = (bf16[3,4,2,128,128]{4,3,2,1,0:T(8,128)(2,1)S(1)}, bf16[3,4,2,128,128]{4,3,2,1,0:T(8,128)(2,1)S(1)}, u32[]{:S(2)}, u32[]{:S(2)}) collective-permute-start(bf16[3,4,2,128,128]{4,3,2,1,0:T(8,128)(2,1)S(1)} %turn.1.ft0), channel_id=1, source_target_pairs={{0,8},{8,0},{1,9},{9,1},{2,10},{10,2},{3,11},{11,3},{4,12},{12,4},... | collective-permute-start | bytes 2359304 | tf_op jit(solution)/shard_map/ppermute | solution.py:24
  85.1 1.0 copy-start.5
  86.1 1.0 copy-start.6
  91.4 1.8 copy-start
  93.2 4.1 %collective-permute-start.10 = (bf16[128,2816]{1,0:T(8,128)(2,1)S(1)}, bf16[128,2816]{1,0:T(8,128)(2,1)S(1)}, u32[]{:S(2)}, u32[]{:S(2)}) collective-permute-start(bf16[128,2816]{1,0:T(8,128)(2,1)S(1)} %get-tuple-element.13.pack.pack0), channel_id=1, source_target_pairs={{0,8},{8,0},{1,9},{9,1},{2,10},{10,2},{3,11},{11,3},{4,12},{12,4},... | collective-permute-start | bytes 2162696 | tf_op jit(solution)/shard_map/ppermute | solution.py:24
  99.8 0.9 copy-start.2
  100.7 20.9 %all-to-all-start.3 = ((bf16[16,16,1792]{2,1,0:T(8,128)(2,1)}), bf16[16,16,1792]{2,1,0:T(8,128)(2,1)}, u32[]{:S(2)}, u32[]{:S(2)}) async-start(bf16[16,16,1792]{2,1,0:T(8,128)(2,1)} %bitcast.3), calls=%async_computation.3 | async-start | bytes 1835008 | tf_op jit(solution)/shard_map/all_to_all | solution.py:155
  107.4 1.1 copy-start.3
  121.7 58.8 %all-to-all-start.2 = ((bf16[16,16,1792]{2,1,0:T(8,128)(2,1)}), bf16[16,16,1792]{2,1,0:T(8,128)(2,1)S(1)}, u32[]{:S(2)}, u32[]{:S(2)}) async-start(bf16[16,16,1792]{2,1,0:T(8,128)(2,1)} %bitcast.2), calls=%async_computation.2 | async-start | bytes 1835008 | tf_op jit(solution)/shard_map/all_to_all | solution.py:155
  127.9 2.0 %copy-start.1 = (bf16[4,256,1792]{2,1,0:T(8,128)(2,1)S(1)}, bf16[4,256,1792]{2,1,0:T(8,128)(2,1)}, u32[]{:S(2)}) copy-start(bf16[4,256,1792]{2,1,0:T(8,128)(2,1)} %copy-done) | copy-start | bytes 11010052
  132.0 26.3 %collective-permute-start.8 = (bf16[128,1024]{1,0:T(8,128)(2,1)S(1)}, bf16[128,1024]{1,0:T(8,128)(2,1)S(1)}, u32[]{:S(2)}, u32[]{:S(2)}) collective-permute-start(bf16[128,1024]{1,0:T(8,128)(2,1)S(1)} %get-tuple-element.18), channel_id=1, source_target_pairs={{0,4},{1,5},{2,6},{3,7},{4,0},{5,1},{6,2},{7,3},{8,12},{9,13},{10,... | collective-permute-start | bytes 786440 | tf_op jit(solution)/shard_map/ppermute | solution.py:20
  138.5 19.8 %collective-permute-start.7 = (bf16[128,1024]{1,0:T(8,128)(2,1)S(1)}, bf16[128,1024]{1,0:T(8,128)(2,1)S(1)}, u32[]{:S(2)}, u32[]{:S(2)}) collective-permute-start(bf16[128,1024]{1,0:T(8,128)(2,1)S(1)} %get-tuple-element.17), channel_id=1, source_target_pairs={{0,2},{1,3},{2,0},{3,1},{4,6},{5,7},{6,4},{7,5},{8,10},{9,11},{10,... | collective-permute-start | bytes 786440 | tf_op jit(solution)/shard_map/ppermute | solution.py:20
  140.4 23.0 %collective-permute-start.6 = (bf16[128,1024]{1,0:T(8,128)(2,1)S(1)}, bf16[128,1024]{1,0:T(8,128)(2,1)S(1)}, u32[]{:S(2)}, u32[]{:S(2)}) collective-permute-start(bf16[128,1024]{1,0:T(8,128)(2,1)S(1)} %get-tuple-element.16), channel_id=1, source_target_pairs={{0,1},{1,0},{2,3},{3,2},{4,5},{5,4},{6,7},{7,6},{8,9},{9,8},{10,11... | collective-permute-start | bytes 786440 | tf_op jit(solution)/shard_map/ppermute | solution.py:20
  165.6 17.0 %collective-permute-start.11 = (bf16[16,1792]{1,0:T(8,128)(2,1)S(1)}, bf16[16,1792]{1,0:T(8,128)(2,1)S(1)}, u32[]{:S(2)}, u32[]{:S(2)}) collective-permute-start(bf16[16,1792]{1,0:T(8,128)(2,1)S(1)} %reduce_sum.22), channel_id=1, source_target_pairs={{0,64},{64,0},{1,65},{65,1},{2,66},{66,2},{3,67},{67,3},{4,68},{68... | collective-permute-start | bytes 172040 | tf_op jit(solution)/shard_map/ppermute | solution.py:24
where the time goes:
time: 184 us; the launch traced here: 183 us
  starting transfers between devices  93.7 us (51%)
  waiting for transfers between devices  63.3 us (34%)
  Pallas kernels  13.7 us (7%)
  local copies, waits for them, and re-layouts  9.36 us (5%)
  other arithmetic  2.32 us (1%)
    ppermute x6, starting transfers between devices, flipped(): return lax.ppermute(block, axis, [(0, 1), (1, 0)])  36.4 us
    ppermute x6, waiting for transfers between devices, swapped(): lax.ppermute(block, 'bfly', [(low, low ^ 1 << stride) for low in range(co...  36.1 us
    ppermute x6, starting transfers between devices, swapped(): lax.ppermute(block, 'bfly', [(low, low ^ 1 << stride) for low in range(co...  29.8 us
    all_to_all x4, starting transfers between devices, exchanged(): return lax.all_to_all(rows, PLANE, split_axis=0, concat_axis=0, tiled=True)  27.6 us
    all_to_all x4, waiting for transfers between devices, exchanged(): return lax.all_to_all(rows, PLANE, split_axis=0, concat_axis=0, tiled=True)  20.7 us
    unnamed x16, local copies, waits for them, and re-layouts  7.8 us
    ppermute x6, waiting for transfers between devices, flipped(): return lax.ppermute(block, axis, [(0, 1), (1, 0)])  6.58 us
    pallas_call x1, Pallas kernels, body(): pl.pallas_call(forward_kernel, out_shape=(jax.ShapeDtypeStruct((tok_rows,...  4.35 us
  transfers between devices with their start and end apart: 16, of which 9 were waited for; matrix products, arithmetic and copies ran while one was open for 1% of the time, Pallas kernels for 6%

commit v1 on v0

--- a/solution.py
+++ b/solution.py
@@ -28,6 +28,14 @@
     return pl.BlockSpec(memory_space=pltpu.VMEM)
 
 
+def hbm():
+    return pl.BlockSpec(memory_space=pltpu.MemorySpace.HBM)
+
+
+def in_hbm(array):
+    return pltpu.with_memory_space_constraint(array, pltpu.MemorySpace.HBM)
+
+
 def smem():
     return pl.BlockSpec(memory_space=pltpu.SMEM)
 
@@ -61,20 +69,23 @@
     return (col == sent).astype(jnp.bfloat16)
 
 
-def forward_kernel(tab, f0, f1, f2, f3, w00, w01, w10, w11, up_hbm, act, pack, wn, up, sem):
+def forward_kernel(tab, g0, g1, g2, g3, w00, w01, w10, w11, up_hbm, act, pack, wn, f0, f1, f2, f3, up, sems):
     feats = (f0, f1, f2, f3)
     sections, hidden_blocks = tab.shape
-    fetch = pltpu.make_async_copy(up_hbm, up, sem)
-    fetch.start()
+    moves = zip((g0, g1, g2, g3, up_hbm), (f0, f1, f2, f3, up), range(5))
+    fetches = [pltpu.make_async_copy(source, target, sems.at[i]) for source, target, i in moves]
+    for fetch in fetches:
+        fetch.start()
     order = gather_order()
     for x in range(XS):
         rows = jnp.concatenate([w00[x], w01[x], w10[x], w11[x]], axis=0)
         ordered = jnp.dot(order, rows, preferred_element_type=jnp.float32).astype(jnp.bfloat16)
         for s in range(sections):
             wn[s, x * 64 : (x + 1) * 64, :] = ordered[s * 64 : (s + 1) * 64]
+    for fetch in fetches:
+        fetch.wait()
     edge = f3.shape[1]
     pack[:, :edge] = f3[...]
-    fetch.wait()
     for j in range(hidden_blocks):
         cols = slice(j * 256, (j + 1) * 256)
         spot = slice(edge + j * 256, edge + (j + 1) * 256)
@@ -200,12 +211,13 @@
             jax.ShapeDtypeStruct((tok_rows, edge + width), bf16),
             jax.ShapeDtypeStruct((sections, 256, width), bf16),
         ),
-        in_specs=[smem()] + [vmem()] * 8 + [pl.BlockSpec(memory_space=pltpu.MemorySpace.HBM)],
+        in_specs=[smem()] + [hbm()] * 4 + [vmem()] * 4 + [hbm()],
         out_specs=(vmem(), vmem(), vmem()),
-        scratch_shapes=[pltpu.VMEM((tok_rows, width), bf16), pltpu.SemaphoreType.DMA],
+        scratch_shapes=[pltpu.VMEM((tok_rows, edge), bf16)] * 4
+        + [pltpu.VMEM((tok_rows, width), bf16), pltpu.SemaphoreType.DMA((5,))],
         compiler_params=params(),
         name="forward",
-    )(block_table, *feats, w00, w01, w10, w11, upstream)
+    )(block_table, *map(in_hbm, feats), w00, w01, w10, w11, in_hbm(upstream))
     pack_got = flipped(pack, "core")
 
     share = jax.ShapeDtypeStruct((tok_rows, edge), bf16)

time: 184 us -> 184 us (level)
    unnamed x16 -> x18, local copies, waits for them, and re-layouts: 7.8 us -> 6.54 us
where the time goes in v1:
time: 184 us; the launch traced here: 183 us
  starting transfers between devices  93.7 us (51%)
  waiting for transfers between devices  63.4 us (34%)
  Pallas kernels  14.5 us (8%)
  local copies, waits for them, and re-layouts  8.1 us (4%)
  other arithmetic  2.32 us (1%)
    ppermute x6, starting transfers between devices, flipped(): return lax.ppermute(block, axis, [(0, 1), (1, 0)])  36.4 us
    ppermute x6, waiting for transfers between devices, swapped(): lax.ppermute(block, 'bfly', [(low, low ^ 1 << stride) for low in range(co...  36.1 us
    ppermute x6, starting transfers between devices, swapped(): lax.ppermute(block, 'bfly', [(low, low ^ 1 << stride) for low in range(co...  29.8 us
    all_to_all x4, starting transfers between devices, exchanged(): return lax.all_to_all(rows, PLANE, split_axis=0, concat_axis=0, tiled=True)  27.6 us
    all_to_all x4, waiting for transfers between devices, exchanged(): return lax.all_to_all(rows, PLANE, split_axis=0, concat_axis=0, tiled=True)  20.7 us
    ppermute x6, waiting for transfers between devices, flipped(): return lax.ppermute(block, axis, [(0, 1), (1, 0)])  6.58 us
    unnamed x18, local copies, waits for them, and re-layouts  6.54 us
    pallas_call x1, Pallas kernels, body(): pl.pallas_call(forward_kernel, out_shape=(jax.ShapeDtypeStruct((tok_rows,...  5.14 us
  transfers between devices with their start and end apart: 16, of which 9 were waited for; matrix products, arithmetic and copies ran while one was open for 1% of the time, Pallas kernels for 6%

profile of v1, /device:TPU:66, one launch (start us, length us, event | category | flops | bytes accessed | tf_op | source)
XLA Modules:
  0.0 182.8 jit_solution(1193100379352686123)
XLA Ops:
  0.6 0.0 copy-start.4
  0.6 0.0 copy-start.7
  0.7 0.9 reshape.24.shard
  1.5 1.0 repeat.2
  2.5 7.5 %all-to-all-start = ((bf16[16,16,1792]{2,1,0:T(8,128)(2,1)}), bf16[16,16,1792]{2,1,0:T(8,128)(2,1)S(1)}, u32[]{:S(2)}, u32[]{:S(2)}) async-start(bf16[16,16,1792]{2,1,0:T(8,128)(2,1)} %repeat.2), calls=%async_computation | async-start | bytes 1835008 | tf_op jit(solution)/shard_map/all_to_all | solution.py:166
  10.0 13.9 %collective-permute-start.3 = (bf16[16,1792]{1,0:T(8,128)(2,1)S(1)}, bf16[16,1792]{1,0:T(8,128)(2,1)S(1)}, u32[]{:S(2)}, u32[]{:S(2)}) collective-permute-start(bf16[16,1792]{1,0:T(8,128)(2,1)S(1)} %reshape.24.shard), channel_id=1, source_target_pairs={{0,64},{64,0},{1,65},{65,1},{2,66},{66,2},{3,67},{67,3},{4,68},{68... | collective-permute-start | bytes 172040 | tf_op jit(solution)/shard_map/ppermute | solution.py:24
  23.9 2.4 %collective-permute-done.3.shard = bf16[16,1792]{1,0:T(8,128)(2,1)S(1)} collective-permute-done((bf16[16,1792]{1,0:T(8,128)(2,1)S(1)}, bf16[16,1792]{1,0:T(8,128)(2,1)S(1)}, u32[]{:S(2)}, u32[]{:S(2)}) %collective-permute-start.3) | collective-permute-done | bytes 57376 | tf_op jit(solution)/shard_map/ppermute | solution.py:24
  26.4 1.0 repeat.3
  27.4 0.0 all-to-all-done
  27.4 7.2 %all-to-all-start.1 = ((bf16[16,16,1792]{2,1,0:T(8,128)(2,1)}), bf16[16,16,1792]{2,1,0:T(8,128)(2,1)S(1)}, u32[]{:S(2)}, u32[]{:S(2)}) async-start(bf16[16,16,1792]{2,1,0:T(8,128)(2,1)} %repeat.3), calls=%async_computation.1 | async-start | bytes 1835008 | tf_op jit(solution)/shard_map/all_to_all | solution.py:166
  34.6 1.9 %collective-permute-start.4 = (bf16[4,64,1792]{2,1,0:T(8,128)(2,1)S(1)}, bf16[4,64,1792]{2,1,0:T(8,128)(2,1)}, u32[]{:S(2)}, u32[]{:S(2)}) collective-permute-start(bf16[4,64,1792]{2,1,0:T(8,128)(2,1)S(1)} %bitcast.4), channel_id=1, source_target_pairs={{0,8},{8,0},{1,9},{9,1},{2,10},{10,2},{3,11},{11,3},{4,12},{12,4},... | collective-permute-start | bytes 2752520 | tf_op jit(solution)/shard_map/ppermute | solution.py:24
  36.5 10.0 %all-to-all-done.1 = bf16[16,16,1792]{2,1,0:T(8,128)(2,1)S(1)} async-done(((bf16[16,16,1792]{2,1,0:T(8,128)(2,1)}), bf16[16,16,1792]{2,1,0:T(8,128)(2,1)S(1)}, u32[]{:S(2)}, u32[]{:S(2)}) %all-to-all-start.1) | async-done | bytes 917536 | tf_op jit(solution)/shard_map/all_to_all | solution.py:166
  46.5 1.9 %collective-permute-start.5 = (bf16[4,64,1792]{2,1,0:T(8,128)(2,1)S(1)}, bf16[4,64,1792]{2,1,0:T(8,128)(2,1)S(1)}, u32[]{:S(2)}, u32[]{:S(2)}) collective-permute-start(bf16[4,64,1792]{2,1,0:T(8,128)(2,1)S(1)} %bitcast.6), channel_id=1, source_target_pairs={{0,8},{8,0},{1,9},{9,1},{2,10},{10,2},{3,11},{11,3},{4,12},{12,4},... | collective-permute-start | bytes 2752520 | tf_op jit(solution)/shard_map/ppermute | solution.py:24
  48.4 0.0 copy-done.4
  48.4 3.0 %collective-permute-start = (bf16[128,1024]{1,0:T(8,128)(2,1)S(1)}, bf16[128,1024]{1,0:T(8,128)(2,1)S(1)}, u32[]{:S(2)}, u32[]{:S(2)}) collective-permute-start(bf16[128,1024]{1,0:T(8,128)(2,1)S(1)} %copy-done.4), channel_id=1, source_target_pairs={{0,1},{1,0},{2,3},{3,2},{4,5},{5,4},{6,7},{7,6},{8,9},{9,8},{10,11... | collective-permute-start | bytes 786440 | tf_op jit(solution)/shard_map/ppermute | solution.py:20
  51.5 3.2 %collective-permute-start.1 = (bf16[128,1024]{1,0:T(8,128)(2,1)S(1)}, bf16[128,1024]{1,0:T(8,128)(2,1)S(1)}, u32[]{:S(2)}, u32[]{:S(2)}) collective-permute-start(bf16[128,1024]{1,0:T(8,128)(2,1)S(1)} %copy-done.4), channel_id=1, source_target_pairs={{0,2},{1,3},{2,0},{3,1},{4,6},{5,7},{6,4},{7,5},{8,10},{9,11},{10,... | collective-permute-start | bytes 786440 | tf_op jit(solution)/shard_map/ppermute | solution.py:20
  54.7 8.5 %collective-permute-start.2 = (bf16[128,1024]{1,0:T(8,128)(2,1)S(1)}, bf16[128,1024]{1,0:T(8,128)(2,1)S(1)}, u32[]{:S(2)}, u32[]{:S(2)}) collective-permute-start(bf16[128,1024]{1,0:T(8,128)(2,1)S(1)} %copy-done.4), channel_id=1, source_target_pairs={{0,4},{1,5},{2,6},{3,7},{4,0},{5,1},{6,2},{7,3},{8,12},{9,13},{10,... | collective-permute-start | bytes 786440 | tf_op jit(solution)/shard_map/ppermute | solution.py:20
  63.2 0.0 collective-permute-done.g1.f1
  63.2 0.0 copy-start.5
  63.2 11.4 %collective-permute-done.1.g2.f2 = bf16[128,1024]{1,0:T(8,128)(2,1)S(1)} collective-permute-done((bf16[128,1024]{1,0:T(8,128)(2,1)S(1)}, bf16[128,1024]{1,0:T(8,128)(2,1)S(1)}, u32[]{:S(2)}, u32[]{:S(2)}) %collective-permute-start.1) | collective-permute-done | bytes 262176 | tf_op jit(solution)/shard_map/ppermute | solution.py:20
  74.7 0.0 copy-start.6
  74.7 0.3 turn.1.ft0
  74.9 1.9 %collective-permute-start.9 = (bf16[3,4,2,128,128]{4,3,2,1,0:T(8,128)(2,1)S(1)}, bf16[3,4,2,128,128]{4,3,2,1,0:T(8,128)(2,1)S(1)}, u32[]{:S(2)}, u32[]{:S(2)}) collective-permute-start(bf16[3,4,2,128,128]{4,3,2,1,0:T(8,128)(2,1)S(1)} %turn.1.ft0), channel_id=1, source_target_pairs={{0,8},{8,0},{1,9},{9,1},{2,10},{10,2},{3,11},{11,3},{4,12},{12,4},... | collective-permute-start | bytes 2359304 | tf_op jit(solution)/shard_map/ppermute | solution.py:24
  76.9 8.2 %collective-permute-done.2.g3 = bf16[128,1024]{1,0:T(8,128)(2,1)S(1)} collective-permute-done((bf16[128,1024]{1,0:T(8,128)(2,1)S(1)}, bf16[128,1024]{1,0:T(8,128)(2,1)S(1)}, u32[]{:S(2)}, u32[]{:S(2)}) %collective-permute-start.2) | collective-permute-done | bytes 262176 | tf_op jit(solution)/shard_map/ppermute | solution.py:20
  85.1 0.0 copy-start.8
  85.1 0.0 collective-permute-done.4.w10
  85.1 0.0 collective-permute-done.5.w11
  85.1 0.0 copy-done.5
  85.1 0.0 copy-done.6
  85.1 0.7 copy-done.8
  85.8 0.0 copy-done.7
  85.8 5.1 %forward.1 = (bf16[128,1792]{1,0:T(8,128)(2,1)}, bf16[128,2816]{1,0:T(8,128)(2,1)S(1)}, bf16[4,256,1792]{2,1,0:T(8,128)(2,1)S(1)}) custom-call(s32[4,7]{1,0:T(4,128)S(1)} %copy-done.7, bf16[128,1024]{1,0:T(8,128)(2,1)} %f0.1, bf16[128,1024]{1,0:T(8,128)(2,1)} %copy-done.5, bf16[128,1024]{1,0:T(8,128)(2,1)} %copy-done.6, bf16[128,1024]{1,0:T(8,128)(2,1)} %copy-done.8, ...), custom_call_target="tpu_custom_call" | custom-call | tf_op jit(solution)/shard_map/forward/pallas_call | solution.py:207
  90.9 0.0 copy-start
  91.0 1.8 copy-done
  92.7 1.9 %collective-permute-start.10 = (bf16[128,2816]{1,0:T(8,128)(2,1)S(1)}, bf16[128,2816]{1,0:T(8,128)(2,1)S(1)}, u32[]{:S(2)}, u32[]{:S(2)}) collective-permute-start(bf16[128,2816]{1,0:T(8,128)(2,1)S(1)} %get-tuple-element.13.pack.pack0), channel_id=1, source_target_pairs={{0,8},{8,0},{1,9},{9,1},{2,10},{10,2},{3,11},{11,3},{4,12},{12,4},... | collective-permute-start | bytes 2162696 | tf_op jit(solution)/shard_map/ppermute | solution.py:24
  94.7 0.0 collective-permute-done.9.ft1
  94.7 2.1 %collective-permute-done.10.pack1 = bf16[128,2816]{1,0:T(8,128)(2,1)S(1)} collective-permute-done((bf16[128,2816]{1,0:T(8,128)(2,1)S(1)}, bf16[128,2816]{1,0:T(8,128)(2,1)S(1)}, u32[]{:S(2)}, u32[]{:S(2)}) %collective-permute-start.10) | collective-permute-done | bytes 720928 | tf_op jit(solution)/shard_map/ppermute | solution.py:24
  96.8 2.5 %far_rows.1 = (bf16[2,128,1792]{2,1,0:T(8,128)(2,1)}, bf16[4,2,128,256]{3,2,1,0:T(8,128)(2,1)S(1)}) custom-call(s32[4,7]{1,0:T(4,128)S(1)} %copy-done.7, bf16[3,4,2,128,128]{4,3,2,1,0:T(8,128)(2,1)S(1)} %turn.1.ft0, bf16[3,4,2,128,128]{4,3,2,1,0:T(8,128)(2,1)S(1)} %collective-permute-done.9.ft1, bf16[128,2816]{1,0:T(8,128)(2,1)S(1)} %get-tuple-element.13.pack.pack0, ...), custom_call_target="tpu_custom_call" | custom-call | tf_op jit(solution)/shard_map/far_rows/pallas_call | solution.py:237
  99.4 0.0 copy-start.2
  99.4 0.9 copy-done.2
  100.3 6.7 %all-to-all-start.3 = ((bf16[16,16,1792]{2,1,0:T(8,128)(2,1)}), bf16[16,16,1792]{2,1,0:T(8,128)(2,1)}, u32[]{:S(2)}, u32[]{:S(2)}) async-start(bf16[16,16,1792]{2,1,0:T(8,128)(2,1)} %bitcast.3), calls=%async_computation.3 | async-start | bytes 1835008 | tf_op jit(solution)/shard_map/all_to_all | solution.py:166
  106.9 0.0 copy-start.3
  106.9 1.1 copy-done.3
  108.1 2.4 %near_rows.1 = bf16[2,128,1792]{2,1,0:T(8,128)(2,1)} custom-call(s32[4,7]{1,0:T(4,128)S(1)} %copy-done.7, bf16[3,4,2,128,128]{4,3,2,1,0:T(8,128)(2,1)S(1)} %turn.1.ft0, bf16[3,4,2,128,128]{4,3,2,1,0:T(8,128)(2,1)S(1)} %copy-done.3, bf16[4,2,128,256]{3,2,1,0:T(8,128)(2,1)S(1)} %get-tuple-element.19.last, bf16[128,2816]{1,0:T(8,128)(2,1)S(1)} %get-tuple-element.13.pack.pack0, ...), custom_call_target="tpu_custom_call" | custom-call | tf_op jit(solution)/shard_map/near_rows/pallas_call | solution.py:247
  110.5 10.7 %all-to-all-done.3 = bf16[16,16,1792]{2,1,0:T(8,128)(2,1)} async-done(((bf16[16,16,1792]{2,1,0:T(8,128)(2,1)}), bf16[16,16,1792]{2,1,0:T(8,128)(2,1)}, u32[]{:S(2)}, u32[]{:S(2)}) %all-to-all-start.3) | async-done | bytes 917536 | tf_op jit(solution)/shard_map/all_to_all | solution.py:166
  121.2 6.2 %all-to-all-start.2 = ((bf16[16,16,1792]{2,1,0:T(8,128)(2,1)}), bf16[16,16,1792]{2,1,0:T(8,128)(2,1)S(1)}, u32[]{:S(2)}, u32[]{:S(2)}) async-start(bf16[16,16,1792]{2,1,0:T(8,128)(2,1)} %bitcast.2), calls=%async_computation.2 | async-start | bytes 1835008 | tf_op jit(solution)/shard_map/all_to_all | solution.py:166
  127.4 0.0 copy-start.1
  127.4 2.0 %copy-done.1 = bf16[4,256,1792]{2,1,0:T(8,128)(2,1)S(1)} copy-done((bf16[4,256,1792]{2,1,0:T(8,128)(2,1)S(1)}, bf16[4,256,1792]{2,1,0:T(8,128)(2,1)}, u32[]{:S(2)}) %copy-start.1) | copy-done | bytes 3670040
  129.4 2.1 %shares.1 = (bf16[128,1024]{1,0:T(8,128)(2,1)S(1)}, bf16[128,1024]{1,0:T(8,128)(2,1)S(1)}, bf16[128,1024]{1,0:T(8,128)(2,1)S(1)}, bf16[128,1024]{1,0:T(8,128)(2,1)S(1)}) custom-call(s32[4,7]{1,0:T(4,128)S(1)} %copy-done.7, bf16[128,2816]{1,0:T(8,128)(2,1)S(1)} %get-tuple-element.13.pack.pack0, bf16[4,256,1792]{2,1,0:T(8,128)(2,1)S(1)} %copy-done.1), custom_call_target="tpu_custom_call" | custom-call | tf_op jit(solution)/shard_map/shares/pallas_call | solution.py:224
  131.5 6.5 %collective-permute-start.8 = (bf16[128,1024]{1,0:T(8,128)(2,1)S(1)}, bf16[128,1024]{1,0:T(8,128)(2,1)S(1)}, u32[]{:S(2)}, u32[]{:S(2)}) collective-permute-start(bf16[128,1024]{1,0:T(8,128)(2,1)S(1)} %get-tuple-element.18), channel_id=1, source_target_pairs={{0,4},{1,5},{2,6},{3,7},{4,0},{5,1},{6,2},{7,3},{8,12},{9,13},{10,... | collective-permute-start | bytes 786440 | tf_op jit(solution)/shard_map/ppermute | solution.py:20
  138.0 1.9 %collective-permute-start.7 = (bf16[128,1024]{1,0:T(8,128)(2,1)S(1)}, bf16[128,1024]{1,0:T(8,128)(2,1)S(1)}, u32[]{:S(2)}, u32[]{:S(2)}) collective-permute-start(bf16[128,1024]{1,0:T(8,128)(2,1)S(1)} %get-tuple-element.17), channel_id=1, source_target_pairs={{0,2},{1,3},{2,0},{3,1},{4,6},{5,7},{6,4},{7,5},{8,10},{9,11},{10,... | collective-permute-start | bytes 786440 | tf_op jit(solution)/shard_map/ppermute | solution.py:20
  139.9 6.6 %collective-permute-start.6 = (bf16[128,1024]{1,0:T(8,128)(2,1)S(1)}, bf16[128,1024]{1,0:T(8,128)(2,1)S(1)}, u32[]{:S(2)}, u32[]{:S(2)}) collective-permute-start(bf16[128,1024]{1,0:T(8,128)(2,1)S(1)} %get-tuple-element.16), channel_id=1, source_target_pairs={{0,1},{1,0},{2,3},{3,2},{4,5},{5,4},{6,7},{7,6},{8,9},{9,8},{10,11... | collective-permute-start | bytes 786440 | tf_op jit(solution)/shard_map/ppermute | solution.py:20
  146.6 11.3 %collective-permute-done.8 = bf16[128,1024]{1,0:T(8,128)(2,1)S(1)} collective-permute-done((bf16[128,1024]{1,0:T(8,128)(2,1)S(1)}, bf16[128,1024]{1,0:T(8,128)(2,1)S(1)}, u32[]{:S(2)}, u32[]{:S(2)}) %collective-permute-start.8) | collective-permute-done | bytes 262176 | tf_op jit(solution)/shard_map/ppermute | solution.py:20
  157.9 0.0 collective-permute-done.7
  157.9 5.1 %collective-permute-done.6 = bf16[128,1024]{1,0:T(8,128)(2,1)S(1)} collective-permute-done((bf16[128,1024]{1,0:T(8,128)(2,1)S(1)}, bf16[128,1024]{1,0:T(8,128)(2,1)S(1)}, u32[]{:S(2)}, u32[]{:S(2)}) %collective-permute-start.6) | collective-permute-done | bytes 262176 | tf_op jit(solution)/shard_map/ppermute | solution.py:20
  163.0 0.9 add_convert_fusion
  163.8 1.3 reduce_sum.22
  165.1 14.8 %collective-permute-start.11 = (bf16[16,1792]{1,0:T(8,128)(2,1)S(1)}, bf16[16,1792]{1,0:T(8,128)(2,1)S(1)}, u32[]{:S(2)}, u32[]{:S(2)}) collective-permute-start(bf16[16,1792]{1,0:T(8,128)(2,1)S(1)} %reduce_sum.22), channel_id=1, source_target_pairs={{0,64},{64,0},{1,65},{65,1},{2,66},{66,2},{3,67},{67,3},{4,68},{68... | collective-permute-start | bytes 172040 | tf_op jit(solution)/shard_map/ppermute | solution.py:24
  180.0 0.0 all-to-all-done.2
  180.0 0.1 convert_reduce_fusion
  180.1 2.0 %collective-permute-done.11 = bf16[16,1792]{1,0:T(8,128)(2,1)S(1)} collective-permute-done((bf16[16,1792]{1,0:T(8,128)(2,1)S(1)}, bf16[16,1792]{1,0:T(8,128)(2,1)S(1)}, u32[]{:S(2)}, u32[]{:S(2)}) %collective-permute-start.11) | collective-permute-done | bytes 57376 | tf_op jit(solution)/shard_map/ppermute | solution.py:24
  182.2 0.7 reshape.29
  (1 shorter events, 0.0 us)
Async XLA Ops:
  0.6 47.8 %copy-start.4 = (bf16[128,1024]{1,0:T(8,128)(2,1)S(1)}, bf16[128,1024]{1,0:T(8,128)(2,1)}, u32[]{:S(2)}) copy-start(bf16[128,1024]{1,0:T(8,128)(2,1)} %f0.1) | copy-start | bytes 786436
  0.6 85.2 %copy-start.7 = (s32[4,7]{1,0:T(4,128)S(1)}, s32[4,7]{1,0:T(4,128)}, u32[]{:S(2)}) copy-start(s32[4,7]{1,0:T(4,128)} %tab.7) | copy-start | bytes 340
  2.5 24.9 %all-to-all-start = ((bf16[16,16,1792]{2,1,0:T(8,128)(2,1)}), bf16[16,16,1792]{2,1,0:T(8,128)(2,1)S(1)}, u32[]{:S(2)}, u32[]{:S(2)}) async-start(bf16[16,16,1792]{2,1,0:T(8,128)(2,1)} %repeat.2), calls=%async_computation | async-start | bytes 1835008 | tf_op jit(solution)/shard_map/all_to_all | solution.py:166
  10.0 16.4 %collective-permute-start.3 = (bf16[16,1792]{1,0:T(8,128)(2,1)S(1)}, bf16[16,1792]{1,0:T(8,128)(2,1)S(1)}, u32[]{:S(2)}, u32[]{:S(2)}) collective-permute-start(bf16[16,1792]{1,0:T(8,128)(2,1)S(1)} %reshape.24.shard), channel_id=1, source_target_pairs={{0,64},{64,0},{1,65},{65,1},{2,66},{66,2},{3,67},{67,3},{4,68},{68... | collective-permute-start | bytes 172040 | tf_op jit(solution)/shard_map/ppermute | solution.py:24
  27.4 19.1 %all-to-all-start.1 = ((bf16[16,16,1792]{2,1,0:T(8,128)(2,1)}), bf16[16,16,1792]{2,1,0:T(8,128)(2,1)S(1)}, u32[]{:S(2)}, u32[]{:S(2)}) async-start(bf16[16,16,1792]{2,1,0:T(8,128)(2,1)} %repeat.3), calls=%async_computation.1 | async-start | bytes 1835008 | tf_op jit(solution)/shard_map/all_to_all | solution.py:166
  34.6 50.5 %collective-permute-start.4 = (bf16[4,64,1792]{2,1,0:T(8,128)(2,1)S(1)}, bf16[4,64,1792]{2,1,0:T(8,128)(2,1)}, u32[]{:S(2)}, u32[]{:S(2)}) collective-permute-start(bf16[4,64,1792]{2,1,0:T(8,128)(2,1)S(1)} %bitcast.4), channel_id=1, source_target_pairs={{0,8},{8,0},{1,9},{9,1},{2,10},{10,2},{3,11},{11,3},{4,12},{12,4},... | collective-permute-start | bytes 2752520 | tf_op jit(solution)/shard_map/ppermute | solution.py:24
  46.5 38.6 %collective-permute-start.5 = (bf16[4,64,1792]{2,1,0:T(8,128)(2,1)S(1)}, bf16[4,64,1792]{2,1,0:T(8,128)(2,1)S(1)}, u32[]{:S(2)}, u32[]{:S(2)}) collective-permute-start(bf16[4,64,1792]{2,1,0:T(8,128)(2,1)S(1)} %bitcast.6), channel_id=1, source_target_pairs={{0,8},{8,0},{1,9},{9,1},{2,10},{10,2},{3,11},{11,3},{4,12},{12,4},... | collective-permute-start | bytes 2752520 | tf_op jit(solution)/shard_map/ppermute | solution.py:24
  48.4 14.8 %collective-permute-start = (bf16[128,1024]{1,0:T(8,128)(2,1)S(1)}, bf16[128,1024]{1,0:T(8,128)(2,1)S(1)}, u32[]{:S(2)}, u32[]{:S(2)}) collective-permute-start(bf16[128,1024]{1,0:T(8,128)(2,1)S(1)} %copy-done.4), channel_id=1, source_target_pairs={{0,1},{1,0},{2,3},{3,2},{4,5},{5,4},{6,7},{7,6},{8,9},{9,8},{10,11... | collective-permute-start | bytes 786440 | tf_op jit(solution)/shard_map/ppermute | solution.py:20
  51.5 23.2 %collective-permute-start.1 = (bf16[128,1024]{1,0:T(8,128)(2,1)S(1)}, bf16[128,1024]{1,0:T(8,128)(2,1)S(1)}, u32[]{:S(2)}, u32[]{:S(2)}) collective-permute-start(bf16[128,1024]{1,0:T(8,128)(2,1)S(1)} %copy-done.4), channel_id=1, source_target_pairs={{0,2},{1,3},{2,0},{3,1},{4,6},{5,7},{6,4},{7,5},{8,10},{9,11},{10,... | collective-permute-start | bytes 786440 | tf_op jit(solution)/shard_map/ppermute | solution.py:20
  54.7 30.4 %collective-permute-start.2 = (bf16[128,1024]{1,0:T(8,128)(2,1)S(1)}, bf16[128,1024]{1,0:T(8,128)(2,1)S(1)}, u32[]{:S(2)}, u32[]{:S(2)}) collective-permute-start(bf16[128,1024]{1,0:T(8,128)(2,1)S(1)} %copy-done.4), channel_id=1, source_target_pairs={{0,4},{1,5},{2,6},{3,7},{4,0},{5,1},{6,2},{7,3},{8,12},{9,13},{10,... | collective-permute-start | bytes 786440 | tf_op jit(solution)/shard_map/ppermute | solution.py:20
  63.2 21.9 %copy-start.5 = (bf16[128,1024]{1,0:T(8,128)(2,1)}, bf16[128,1024]{1,0:T(8,128)(2,1)S(1)}, u32[]{:S(2)}) copy-start(bf16[128,1024]{1,0:T(8,128)(2,1)S(1)} %collective-permute-done.g1.f1) | copy-start | bytes 786436
  74.7 10.4 %copy-start.6 = (bf16[128,1024]{1,0:T(8,128)(2,1)}, bf16[128,1024]{1,0:T(8,128)(2,1)S(1)}, u32[]{:S(2)}) copy-start(bf16[128,1024]{1,0:T(8,128)(2,1)S(1)} %collective-permute-done.1.g2.f2) | copy-start | bytes 786436
  74.9 19.7 %collective-permute-start.9 = (bf16[3,4,2,128,128]{4,3,2,1,0:T(8,128)(2,1)S(1)}, bf16[3,4,2,128,128]{4,3,2,1,0:T(8,128)(2,1)S(1)}, u32[]{:S(2)}, u32[]{:S(2)}) collective-permute-start(bf16[3,4,2,128,128]{4,3,2,1,0:T(8,128)(2,1)S(1)} %turn.1.ft0), channel_id=1, source_target_pairs={{0,8},{8,0},{1,9},{9,1},{2,10},{10,2},{3,11},{11,3},{4,12},{12,4},... | collective-permute-start | bytes 2359304 | tf_op jit(solution)/shard_map/ppermute | solution.py:24
  85.1 0.7 copy-start.8
  90.9 1.8 copy-start
  92.7 4.1 %collective-permute-start.10 = (bf16[128,2816]{1,0:T(8,128)(2,1)S(1)}, bf16[128,2816]{1,0:T(8,128)(2,1)S(1)}, u32[]{:S(2)}, u32[]{:S(2)}) collective-permute-start(bf16[128,2816]{1,0:T(8,128)(2,1)S(1)} %get-tuple-element.13.pack.pack0), channel_id=1, source_target_pairs={{0,8},{8,0},{1,9},{9,1},{2,10},{10,2},{3,11},{11,3},{4,12},{12,4},... | collective-permute-start | bytes 2162696 | tf_op jit(solution)/shard_map/ppermute | solution.py:24
  99.4 0.9 copy-start.2
  100.3 21.0 %all-to-all-start.3 = ((bf16[16,16,1792]{2,1,0:T(8,128)(2,1)}), bf16[16,16,1792]{2,1,0:T(8,128)(2,1)}, u32[]{:S(2)}, u32[]{:S(2)}) async-start(bf16[16,16,1792]{2,1,0:T(8,128)(2,1)} %bitcast.3), calls=%async_computation.3 | async-start | bytes 1835008 | tf_op jit(solution)/shard_map/all_to_all | solution.py:166
  106.9 1.1 copy-start.3
  121.2 58.8 %all-to-all-start.2 = ((bf16[16,16,1792]{2,1,0:T(8,128)(2,1)}), bf16[16,16,1792]{2,1,0:T(8,128)(2,1)S(1)}, u32[]{:S(2)}, u32[]{:S(2)}) async-start(bf16[16,16,1792]{2,1,0:T(8,128)(2,1)} %bitcast.2), calls=%async_computation.2 | async-start | bytes 1835008 | tf_op jit(solution)/shard_map/all_to_all | solution.py:166
  127.4 2.0 %copy-start.1 = (bf16[4,256,1792]{2,1,0:T(8,128)(2,1)S(1)}, bf16[4,256,1792]{2,1,0:T(8,128)(2,1)}, u32[]{:S(2)}) copy-start(bf16[4,256,1792]{2,1,0:T(8,128)(2,1)} %copy-done) | copy-start | bytes 11010052
  131.5 26.3 %collective-permute-start.8 = (bf16[128,1024]{1,0:T(8,128)(2,1)S(1)}, bf16[128,1024]{1,0:T(8,128)(2,1)S(1)}, u32[]{:S(2)}, u32[]{:S(2)}) collective-permute-start(bf16[128,1024]{1,0:T(8,128)(2,1)S(1)} %get-tuple-element.18), channel_id=1, source_target_pairs={{0,4},{1,5},{2,6},{3,7},{4,0},{5,1},{6,2},{7,3},{8,12},{9,13},{10,... | collective-permute-start | bytes 786440 | tf_op jit(solution)/shard_map/ppermute | solution.py:20
  138.0 19.8 %collective-permute-start.7 = (bf16[128,1024]{1,0:T(8,128)(2,1)S(1)}, bf16[128,1024]{1,0:T(8,128)(2,1)S(1)}, u32[]{:S(2)}, u32[]{:S(2)}) collective-permute-start(bf16[128,1024]{1,0:T(8,128)(2,1)S(1)} %get-tuple-element.17), channel_id=1, source_target_pairs={{0,2},{1,3},{2,0},{3,1},{4,6},{5,7},{6,4},{7,5},{8,10},{9,11},{10,... | collective-permute-start | bytes 786440 | tf_op jit(solution)/shard_map/ppermute | solution.py:20
  139.9 23.0 %collective-permute-start.6 = (bf16[128,1024]{1,0:T(8,128)(2,1)S(1)}, bf16[128,1024]{1,0:T(8,128)(2,1)S(1)}, u32[]{:S(2)}, u32[]{:S(2)}) collective-permute-start(bf16[128,1024]{1,0:T(8,128)(2,1)S(1)} %get-tuple-element.16), channel_id=1, source_target_pairs={{0,1},{1,0},{2,3},{3,2},{4,5},{5,4},{6,7},{7,6},{8,9},{9,8},{10,11... | collective-permute-start | bytes 786440 | tf_op jit(solution)/shard_map/ppermute | solution.py:20
  165.1 17.0 %collective-permute-start.11 = (bf16[16,1792]{1,0:T(8,128)(2,1)S(1)}, bf16[16,1792]{1,0:T(8,128)(2,1)S(1)}, u32[]{:S(2)}, u32[]{:S(2)}) collective-permute-start(bf16[16,1792]{1,0:T(8,128)(2,1)S(1)} %reduce_sum.22), channel_id=1, source_target_pairs={{0,64},{64,0},{1,65},{65,1},{2,66},{66,2},{3,67},{67,3},{4,68},{68... | collective-permute-start | bytes 172040 | tf_op jit(solution)/shard_map/ppermute | solution.py:24
